TPU v7x, 32 devices: a whole 2x2x4 slice. The times are simulated.
32 devices in a mesh: pipe: 4 (over y, x), dp: 8 (over z, core).
Axes of the slice: x: 2, y: 2, z: 4, core: 2. Of those that a mesh axis runs over, the one named last changes fastest.
Arguments:
- inputs: bfloat16 [8, 4, 32, 8192], P('dp'), may hold values from -48 to 48
- segments: int32 [8, 4, 32], P('dp'), may hold values from 0 to 3, never falling along the last dimension, each value on 1 to 16 neighbouring positions
- cotangent: bfloat16 [8, 4, 32, 8192], P('dp'), may hold values from -6 to 6
- w_query: bfloat16 [4, 8192, 128], P('pipe', 'dp'), may hold values from -3 to 3
- w_key: bfloat16 [4, 8192, 128], P('pipe', 'dp'), may hold values from -3 to 3
- w_value: bfloat16 [4, 8192, 128], P('pipe', 'dp'), may hold values from -0.0625 to 0.0625
- w_out: bfloat16 [4, 8192, 128], P('pipe', 'dp'), may hold values from -0.5 to 0.5
Outputs:
- input_grads: bfloat16 [4, 8, 4, 32, 8192], P('pipe', 'dp')
- grad_query: float32 [4, 8192, 128], P('pipe', 'dp')
- grad_key: float32 [4, 8192, 128], P('pipe', 'dp')
- grad_value: float32 [4, 8192, 128], P('pipe', 'dp')
- grad_out: float32 [4, 8192, 128], P('pipe', 'dp')
Inputs may be any that keep to these rules, and one draw needn't show every extreme that they name: `segments`: along each micro-batch the numbers never fall; a document has 1 to 16 tokens, and one has exactly 16.
All inputs are finite; a program needn't handle non-finite values.
Results may differ from a plain program's by a relative error of at most 0.025.
Values may be sent and summed in bfloat16 or wider, within the bound.
No kernel may reach another device: no remote copies, remote signals or barrier semaphores. Data moves between devices by JAX's collectives and lax.ppermute only.
A program may use at most 192 MiB of HBM per device.

v0:
```python
import jax
import jax.numpy as jnp
from jax import lax
from jax.sharding import PartitionSpec as P


def shifted(block, axis, distance):
    devices = range(lax.axis_size(axis))
    route = [(i - distance, i) for i in devices if i - distance in devices]
    return lax.ppermute(block, axis, route)


def section(hidden, doc_ids, w_query, w_key, w_value, w_out):
    widen = hidden.astype(jnp.float32)
    normed = (widen * lax.rsqrt(jnp.mean(widen * widen, axis=-1, keepdims=True) + 1e-05)).astype(
        jnp.bfloat16
    )
    query = jnp.dot(normed, w_query, preferred_element_type=jnp.float32).astype(jnp.bfloat16)
    keys = jnp.dot(normed, w_key, preferred_element_type=jnp.float32).astype(jnp.bfloat16)
    values = jnp.dot(normed, w_value, preferred_element_type=jnp.float32).astype(jnp.bfloat16)
    scores = jnp.dot(query, keys.T, preferred_element_type=jnp.float32) * w_query.shape[1] ** (-0.5)
    places = jnp.arange(hidden.shape[0])
    allowed = (places[:, None] >= places[None, :]) & (doc_ids[:, None] == doc_ids[None, :])
    scores = jnp.where(allowed, scores, -1e30)
    highest = jnp.max(scores, axis=-1, keepdims=True)
    exponent = jnp.where(allowed, jnp.exp(scores - highest), 0.0)
    attend = (exponent / jnp.sum(exponent, axis=-1, keepdims=True)).astype(jnp.bfloat16)
    mixed = jnp.dot(attend, values, preferred_element_type=jnp.float32).astype(jnp.bfloat16)
    update = jnp.dot(mixed, w_out.T, preferred_element_type=jnp.float32)
    return (widen + update).astype(jnp.bfloat16)


def shards(inputs, segments, cotangent, w_query, w_key, w_value, w_out):
    sections = lax.axis_size("pipe")
    section_id = lax.axis_index("pipe")
    full_query, full_key, full_value, full_out = (
        lax.all_gather(w_query, "dp", axis=1, tiled=True),
        lax.all_gather(w_key, "dp", axis=1, tiled=True),
        lax.all_gather(w_value, "dp", axis=1, tiled=True),
        lax.all_gather(w_out, "dp", axis=1, tiled=True),
    )
    layer = (full_query[0], full_key[0], full_value[0], full_out[0])
    features = inputs[0]
    doc_table = segments[0]
    final_cots = cotangent[0]
    batches = features.shape[0]
    ticks = sections + batches - 1

    def forward_tick(tick, carry):
        incoming, stash = carry
        offset = tick - section_id
        active = (offset >= 0) & (offset < batches)
        batch_slot = jnp.clip(offset, 0, batches - 1)
        first = lax.dynamic_index_in_dim(features, batch_slot, 0, keepdims=False)
        section_input = jnp.where(section_id == 0, first, incoming)
        doc_ids = lax.dynamic_index_in_dim(doc_table, batch_slot, 0, keepdims=False)
        result = lax.cond(
            active,
            lambda: section(section_input, doc_ids, *layer),
            lambda: jnp.zeros_like(section_input),
        )
        previous = lax.dynamic_index_in_dim(stash, batch_slot, 0, keepdims=False)
        stash = lax.dynamic_update_index_in_dim(
            stash, jnp.where(active, section_input, previous), batch_slot, 0
        )
        incoming = shifted(result, "pipe", 1)
        return (incoming, stash)

    start_buffer = jnp.zeros(features.shape[1:], jnp.bfloat16)
    _, stash = lax.fori_loop(0, ticks, forward_tick, (start_buffer, jnp.zeros_like(features)))

    def backward_tick(tick, carry):
        incoming, totals, stored = carry
        offset = tick - (sections - 1 - section_id)
        active = (offset >= 0) & (offset < batches)
        batch_slot = jnp.clip(offset, 0, batches - 1)
        last_cot = lax.dynamic_index_in_dim(final_cots, batch_slot, 0, keepdims=False)
        grad_input = jnp.where(section_id == sections - 1, last_cot, incoming)
        saved_h = lax.dynamic_index_in_dim(stash, batch_slot, 0, keepdims=False)
        doc_ids = lax.dynamic_index_in_dim(doc_table, batch_slot, 0, keepdims=False)

        def run_back():
            _, pull = jax.vjp(
                lambda hid, wa, wb, wc, wd: section(hid, doc_ids, wa, wb, wc, wd), saved_h, *layer
            )
            outs = pull(grad_input)
            return (outs[0], tuple((grad.astype(jnp.float32) for grad in outs[1:])))

        def skip_back():
            return (
                jnp.zeros_like(saved_h),
                tuple((jnp.zeros(part.shape, jnp.float32) for part in layer)),
            )

        cot_input, parts = lax.cond(active, run_back, skip_back)
        totals = tuple((total + part for total, part in zip(totals, parts)))
        previous = lax.dynamic_index_in_dim(stored, batch_slot, 0, keepdims=False)
        stored = lax.dynamic_update_index_in_dim(
            stored, jnp.where(active, cot_input, previous), batch_slot, 0
        )
        incoming = shifted(cot_input, "pipe", -1)
        return (incoming, totals, stored)

    zero_totals = tuple((jnp.zeros(part.shape, jnp.float32) for part in layer))
    _, totals, stored = lax.fori_loop(
        0, ticks, backward_tick, (start_buffer, zero_totals, jnp.zeros_like(features))
    )
    owned_grads = (
        lax.psum_scatter(
            totals[0].astype(jnp.bfloat16)[None], "dp", scatter_dimension=1, tiled=True
        ).astype(jnp.float32),
        lax.psum_scatter(
            totals[1].astype(jnp.bfloat16)[None], "dp", scatter_dimension=1, tiled=True
        ).astype(jnp.float32),
        lax.psum_scatter(
            totals[2].astype(jnp.bfloat16)[None], "dp", scatter_dimension=1, tiled=True
        ).astype(jnp.float32),
        lax.psum_scatter(
            totals[3].astype(jnp.bfloat16)[None], "dp", scatter_dimension=1, tiled=True
        ).astype(jnp.float32),
    )
    return (stored[None, None], owned_grads[0], owned_grads[1], owned_grads[2], owned_grads[3])


def solution(mesh):
    placed = (
        P("dp", None, None, None),
        P("dp", None, None),
        P("dp", None, None, None),
        P("pipe", "dp", None),
        P("pipe", "dp", None),
        P("pipe", "dp", None),
        P("pipe", "dp", None),
    )
    return jax.shard_map(
        shards,
        mesh=mesh,
        in_specs=placed,
        out_specs=(
            P("pipe", "dp", None, None, None),
            P("pipe", "dp", None),
            P("pipe", "dp", None),
            P("pipe", "dp", None),
            P("pipe", "dp", None),
        ),
        check_vma=False,
    )
```

profile of v0, /device:TPU:0, one launch (start us, length us, event | category | flops | bytes accessed | tf_op | source)
XLA Modules:
  0.0 771.5 jit_solution(6863091489487590063)
XLA Ops:
  10.1 31.4 %all-gather.5.cloned.1.call-done = bf16[1,8192,128]{2,1,0:T(8,128)(2,1)} async-done(((bf16[1,1024,128]{2,1,0:T(8,128)(2,1)}), bf16[1,8192,128]{2,1,0:T(8,128)(2,1)}) %all-gather.5.cloned.1.call-update) | async-done | bytes 2097168 | tf_op jit(solution)/shard_map/all_gather | solution.py:37
  41.4 30.2 %all-gather.7.cloned.1.call-done = bf16[1,8192,128]{2,1,0:T(8,128)(2,1)} async-done(((bf16[1,1024,128]{2,1,0:T(8,128)(2,1)}), bf16[1,8192,128]{2,1,0:T(8,128)(2,1)}) %all-gather.7.cloned.1.call-update) | async-done | bytes 2097168 | tf_op jit(solution)/shard_map/all_gather | solution.py:38
  71.7 30.2 %all-gather.9.cloned.1.call-done = bf16[1,8192,128]{2,1,0:T(8,128)(2,1)} async-done(((bf16[1,1024,128]{2,1,0:T(8,128)(2,1)}), bf16[1,8192,128]{2,1,0:T(8,128)(2,1)}) %all-gather.9.cloned.1.call-update) | async-done | bytes 2097168 | tf_op jit(solution)/shard_map/all_gather | solution.py:39
  101.9 30.1 %all-gather.11.cloned.1.call-done = bf16[1,8192,128]{2,1,0:T(8,128)(2,1)} async-done(((bf16[1,1024,128]{2,1,0:T(8,128)(2,1)}), bf16[1,8192,128]{2,1,0:T(8,128)(2,1)}) %all-gather.11.cloned.1.call-update) | async-done | bytes 2097168 | tf_op jit(solution)/shard_map/all_gather | solution.py:40
  133.6 171.1 %while.42 = (s32[]{:T(128)}, bf16[32,8192]{1,0:T(8,128)(2,1)S(1)}, bf16[4,32,8192]{2,1,0:T(8,128)(2,1)}, s32[]{:T(128)}, pred[]{:T(512)}, /*index=5*/bf16[4,32,8...) while((s32[]{:T(128)}, bf16[32,8192]{1,0:T(8,128)(2,1)S(1)}, ...), condition=%wide.region_6.7_spmd, body=%wide.region_0.6_spmd.sunk | while | flops 273452000 | bytes 19447128 | solution.py:70
  146.7 12.1 %collective-permute-done = bf16[32,8192]{1,0:T(8,128)(2,1)S(1)} collective-permute-done((bf16[32,8192]{1,0:T(8,128)(2,1)}, bf16[32,8192]{1,0:T(8,128)(2,1)S(1)}, u32[]{:S(2)}, u32[]{:S(2)}) %collective-permute-start) | collective-permute-done | bytes 524320 | tf_op jit(solution)/shard_map/while/body/eval_jaxpr/ppermute | solution.py:10
  174.8 11.3 %collective-permute-done = bf16[32,8192]{1,0:T(8,128)(2,1)S(1)} collective-permute-done((bf16[32,8192]{1,0:T(8,128)(2,1)}, bf16[32,8192]{1,0:T(8,128)(2,1)S(1)}, u32[]{:S(2)}, u32[]{:S(2)}) %collective-permute-start) | collective-permute-done | bytes 524320 | tf_op jit(solution)/shard_map/while/body/eval_jaxpr/ppermute | solution.py:10
  202.1 10.5 %collective-permute-done = bf16[32,8192]{1,0:T(8,128)(2,1)S(1)} collective-permute-done((bf16[32,8192]{1,0:T(8,128)(2,1)}, bf16[32,8192]{1,0:T(8,128)(2,1)S(1)}, u32[]{:S(2)}, u32[]{:S(2)}) %collective-permute-start) | collective-permute-done | bytes 524320 | tf_op jit(solution)/shard_map/while/body/eval_jaxpr/ppermute | solution.py:10
  242.1 12.4 %collective-permute-start = (bf16[32,8192]{1,0:T(8,128)(2,1)}, bf16[32,8192]{1,0:T(8,128)(2,1)S(1)}, u32[]{:S(2)}, u32[]{:S(2)}) collective-permute-start(bf16[32,8192]{1,0:T(8,128)(2,1)} %copy-done.9), channel_id=1, source_target_pairs={{0,8},{8,16},{16,24},{1,9},{9,17},{17,25},{2,10},{10,18},{18,26},{... | collective-permute-start | bytes 1572872 | tf_op jit(solution)/shard_map/while/body/eval_jaxpr/ppermute | solution.py:10
  284.7 12.9 %collective-permute-start = (bf16[32,8192]{1,0:T(8,128)(2,1)}, bf16[32,8192]{1,0:T(8,128)(2,1)S(1)}, u32[]{:S(2)}, u32[]{:S(2)}) collective-permute-start(bf16[32,8192]{1,0:T(8,128)(2,1)} %copy-done.9), channel_id=1, source_target_pairs={{0,8},{8,16},{16,24},{1,9},{9,17},{17,25},{2,10},{10,18},{18,26},{... | collective-permute-start | bytes 1572872 | tf_op jit(solution)/shard_map/while/body/eval_jaxpr/ppermute | solution.py:10
  307.0 305.3 %while.43 = (s32[]{:T(128)}, bf16[32,8192]{1,0:T(8,128)(2,1)}, f32[8192,128]{1,0:T(8,128)}, f32[8192,128]{1,0:T(8,128)}, f32[8192,128]{1,0:T(8,128)}, /*index=5*...) while((s32[]{:T(128)}, bf16[32,8192]{1,0:T(8,128)(2,1)}, ...), condition=%wide.region_17.18_spmd.clone, body=%wide.region_7.17_spmd.clone.sunk | while | flops 767129792 | bytes 153846560 | solution.py:105
  346.4 9.9 %select_add_fusion.7 = (f32[8192,128]{1,0:T(8,128)}, f32[8192,128]{1,0:T(8,128)}) fusion(f32[8192,128]{1,0:T(8,128)} %get-tuple-element.1022, f32[8192,128]{1,0:T(8,128)} %get-tuple-element.1106, pred[]{:T(512)S(6)} %compare.3, f32[8192,128]{1,0:T(8,128)} %get-tuple-element.1023, f32[8192,128]{1,0:T(8,128)} %get-tuple-element.1105), kind=kLoop, calls=%fused_computation.93.clone.1 | loop fusion | flops 4194304 | bytes 25165824 | tf_op jit(solution)/shard_map/while/body/eval_jaxpr/add | solution.py:96
  356.3 9.9 %select_add_fusion.6 = (f32[8192,128]{1,0:T(8,128)}, f32[8192,128]{1,0:T(8,128)}) fusion(f32[8192,128]{1,0:T(8,128)} %get-tuple-element.1018, f32[8192,128]{1,0:T(8,128)} %get-tuple-element.1104, pred[]{:T(512)S(6)} %compare.3, f32[8192,128]{1,0:T(8,128)} %get-tuple-element.1019, f32[8192,128]{1,0:T(8,128)} %get-tuple-element.1103), kind=kLoop, calls=%fused_computation.95.clone.1 | loop fusion | flops 4194304 | bytes 25165824 | tf_op jit(solution)/shard_map/while/body/eval_jaxpr/add | solution.py:96
  379.3 9.9 %select_add_fusion.7 = (f32[8192,128]{1,0:T(8,128)}, f32[8192,128]{1,0:T(8,128)}) fusion(f32[8192,128]{1,0:T(8,128)} %get-tuple-element.1022, f32[8192,128]{1,0:T(8,128)} %get-tuple-element.1106, pred[]{:T(512)S(6)} %compare.3, f32[8192,128]{1,0:T(8,128)} %get-tuple-element.1023, f32[8192,128]{1,0:T(8,128)} %get-tuple-element.1105), kind=kLoop, calls=%fused_computation.93.clone.1 | loop fusion | flops 4194304 | bytes 25165824 | tf_op jit(solution)/shard_map/while/body/eval_jaxpr/add | solution.py:96
  389.2 9.9 %select_add_fusion.6 = (f32[8192,128]{1,0:T(8,128)}, f32[8192,128]{1,0:T(8,128)}) fusion(f32[8192,128]{1,0:T(8,128)} %get-tuple-element.1018, f32[8192,128]{1,0:T(8,128)} %get-tuple-element.1104, pred[]{:T(512)S(6)} %compare.3, f32[8192,128]{1,0:T(8,128)} %get-tuple-element.1019, f32[8192,128]{1,0:T(8,128)} %get-tuple-element.1103), kind=kLoop, calls=%fused_computation.95.clone.1 | loop fusion | flops 4194304 | bytes 25165824 | tf_op jit(solution)/shard_map/while/body/eval_jaxpr/add | solution.py:96
  400.0 19.2 %collective-permute-done.1 = bf16[32,8192]{1,0:T(8,128)(2,1)S(1)} collective-permute-done((bf16[32,8192]{1,0:T(8,128)(2,1)S(1)}, bf16[32,8192]{1,0:T(8,128)(2,1)S(1)}, u32[]{:S(2)}, u32[]{:S(2)}) %collective-permute-start.1) | collective-permute-done | bytes 524320 | tf_op jit(solution)/shard_map/while/body/eval_jaxpr/ppermute | solution.py:10
  420.0 23.7 %conditional.6 = (bf16[32,8192]{1,0:T(8,128)(2,1)S(1)}, f32[8192,128]{1,0:T(8,128)}, f32[8192,128]{1,0:T(8,128)}, f32[8192,128]{1,0:T(8,128)}, f32[8192,128]{1,0:T(8,128)}) conditional(s32[]{:T(128)} %convert_element_type.326, () %tuple.115, (pred[]{:T(512)}, bf16[4,32,8192]{2,1,0:T(8,128)(2,1)}, s32[]{:T(128)}, bf16[32,8192]{1,0:T(8,128)(2,1)}, ...), branch_computations={%region_8.8_spmd, %region_9.16_spmd} | conditional | flops 758479040 | bytes 96698248 | solution.py:95
  446.1 9.9 %select_add_fusion.7 = (f32[8192,128]{1,0:T(8,128)}, f32[8192,128]{1,0:T(8,128)}) fusion(f32[8192,128]{1,0:T(8,128)} %get-tuple-element.1022, f32[8192,128]{1,0:T(8,128)} %get-tuple-element.1106, pred[]{:T(512)S(6)} %compare.3, f32[8192,128]{1,0:T(8,128)} %get-tuple-element.1023, f32[8192,128]{1,0:T(8,128)} %get-tuple-element.1105), kind=kLoop, calls=%fused_computation.93.clone.1 | loop fusion | flops 4194304 | bytes 25165824 | tf_op jit(solution)/shard_map/while/body/eval_jaxpr/add | solution.py:96
  456.0 9.9 %select_add_fusion.6 = (f32[8192,128]{1,0:T(8,128)}, f32[8192,128]{1,0:T(8,128)}) fusion(f32[8192,128]{1,0:T(8,128)} %get-tuple-element.1018, f32[8192,128]{1,0:T(8,128)} %get-tuple-element.1104, pred[]{:T(512)S(6)} %compare.3, f32[8192,128]{1,0:T(8,128)} %get-tuple-element.1019, f32[8192,128]{1,0:T(8,128)} %get-tuple-element.1103), kind=kLoop, calls=%fused_computation.95.clone.1 | loop fusion | flops 4194304 | bytes 25165824 | tf_op jit(solution)/shard_map/while/body/eval_jaxpr/add | solution.py:96
  468.2 23.7 %conditional.6 = (bf16[32,8192]{1,0:T(8,128)(2,1)S(1)}, f32[8192,128]{1,0:T(8,128)}, f32[8192,128]{1,0:T(8,128)}, f32[8192,128]{1,0:T(8,128)}, f32[8192,128]{1,0:T(8,128)}) conditional(s32[]{:T(128)} %convert_element_type.326, () %tuple.115, (pred[]{:T(512)}, bf16[4,32,8192]{2,1,0:T(8,128)(2,1)}, s32[]{:T(128)}, bf16[32,8192]{1,0:T(8,128)(2,1)}, ...), branch_computations={%region_8.8_spmd, %region_9.16_spmd} | conditional | flops 758479040 | bytes 96698248 | solution.py:95
  494.3 9.9 %select_add_fusion.7 = (f32[8192,128]{1,0:T(8,128)}, f32[8192,128]{1,0:T(8,128)}) fusion(f32[8192,128]{1,0:T(8,128)} %get-tuple-element.1022, f32[8192,128]{1,0:T(8,128)} %get-tuple-element.1106, pred[]{:T(512)S(6)} %compare.3, f32[8192,128]{1,0:T(8,128)} %get-tuple-element.1023, f32[8192,128]{1,0:T(8,128)} %get-tuple-element.1105), kind=kLoop, calls=%fused_computation.93.clone.1 | loop fusion | flops 4194304 | bytes 25165824 | tf_op jit(solution)/shard_map/while/body/eval_jaxpr/add | solution.py:96
  504.2 9.9 %select_add_fusion.6 = (f32[8192,128]{1,0:T(8,128)}, f32[8192,128]{1,0:T(8,128)}) fusion(f32[8192,128]{1,0:T(8,128)} %get-tuple-element.1018, f32[8192,128]{1,0:T(8,128)} %get-tuple-element.1104, pred[]{:T(512)S(6)} %compare.3, f32[8192,128]{1,0:T(8,128)} %get-tuple-element.1019, f32[8192,128]{1,0:T(8,128)} %get-tuple-element.1103), kind=kLoop, calls=%fused_computation.95.clone.1 | loop fusion | flops 4194304 | bytes 25165824 | tf_op jit(solution)/shard_map/while/body/eval_jaxpr/add | solution.py:96
  516.5 23.7 %conditional.6 = (bf16[32,8192]{1,0:T(8,128)(2,1)S(1)}, f32[8192,128]{1,0:T(8,128)}, f32[8192,128]{1,0:T(8,128)}, f32[8192,128]{1,0:T(8,128)}, f32[8192,128]{1,0:T(8,128)}) conditional(s32[]{:T(128)} %convert_element_type.326, () %tuple.115, (pred[]{:T(512)}, bf16[4,32,8192]{2,1,0:T(8,128)(2,1)}, s32[]{:T(128)}, bf16[32,8192]{1,0:T(8,128)(2,1)}, ...), branch_computations={%region_8.8_spmd, %region_9.16_spmd} | conditional | flops 758479040 | bytes 96698248 | solution.py:95
  542.5 9.9 %select_add_fusion.7 = (f32[8192,128]{1,0:T(8,128)}, f32[8192,128]{1,0:T(8,128)}) fusion(f32[8192,128]{1,0:T(8,128)} %get-tuple-element.1022, f32[8192,128]{1,0:T(8,128)} %get-tuple-element.1106, pred[]{:T(512)S(6)} %compare.3, f32[8192,128]{1,0:T(8,128)} %get-tuple-element.1023, f32[8192,128]{1,0:T(8,128)} %get-tuple-element.1105), kind=kLoop, calls=%fused_computation.93.clone.1 | loop fusion | flops 4194304 | bytes 25165824 | tf_op jit(solution)/shard_map/while/body/eval_jaxpr/add | solution.py:96
  552.4 9.9 %select_add_fusion.6 = (f32[8192,128]{1,0:T(8,128)}, f32[8192,128]{1,0:T(8,128)}) fusion(f32[8192,128]{1,0:T(8,128)} %get-tuple-element.1018, f32[8192,128]{1,0:T(8,128)} %get-tuple-element.1104, pred[]{:T(512)S(6)} %compare.3, f32[8192,128]{1,0:T(8,128)} %get-tuple-element.1019, f32[8192,128]{1,0:T(8,128)} %get-tuple-element.1103), kind=kLoop, calls=%fused_computation.95.clone.1 | loop fusion | flops 4194304 | bytes 25165824 | tf_op jit(solution)/shard_map/while/body/eval_jaxpr/add | solution.py:96
  564.7 23.7 %conditional.6 = (bf16[32,8192]{1,0:T(8,128)(2,1)S(1)}, f32[8192,128]{1,0:T(8,128)}, f32[8192,128]{1,0:T(8,128)}, f32[8192,128]{1,0:T(8,128)}, f32[8192,128]{1,0:T(8,128)}) conditional(s32[]{:T(128)} %convert_element_type.326, () %tuple.115, (pred[]{:T(512)}, bf16[4,32,8192]{2,1,0:T(8,128)(2,1)}, s32[]{:T(128)}, bf16[32,8192]{1,0:T(8,128)(2,1)}, ...), branch_computations={%region_8.8_spmd, %region_9.16_spmd} | conditional | flops 758479040 | bytes 96698248 | solution.py:95
  590.7 9.9 %select_add_fusion.7 = (f32[8192,128]{1,0:T(8,128)}, f32[8192,128]{1,0:T(8,128)}) fusion(f32[8192,128]{1,0:T(8,128)} %get-tuple-element.1022, f32[8192,128]{1,0:T(8,128)} %get-tuple-element.1106, pred[]{:T(512)S(6)} %compare.3, f32[8192,128]{1,0:T(8,128)} %get-tuple-element.1023, f32[8192,128]{1,0:T(8,128)} %get-tuple-element.1105), kind=kLoop, calls=%fused_computation.93.clone.1 | loop fusion | flops 4194304 | bytes 25165824 | tf_op jit(solution)/shard_map/while/body/eval_jaxpr/add | solution.py:96
  600.7 9.9 %select_add_fusion.6 = (f32[8192,128]{1,0:T(8,128)}, f32[8192,128]{1,0:T(8,128)}) fusion(f32[8192,128]{1,0:T(8,128)} %get-tuple-element.1018, f32[8192,128]{1,0:T(8,128)} %get-tuple-element.1104, pred[]{:T(512)S(6)} %compare.3, f32[8192,128]{1,0:T(8,128)} %get-tuple-element.1019, f32[8192,128]{1,0:T(8,128)} %get-tuple-element.1103), kind=kLoop, calls=%fused_computation.95.clone.1 | loop fusion | flops 4194304 | bytes 25165824 | tf_op jit(solution)/shard_map/while/body/eval_jaxpr/add | solution.py:96
  627.4 25.3 %reduce-scatter.5.cloned.1.call-done = bf16[1,1024,128]{2,1,0:T(8,128)(2,1)} async-done(((bf16[1,8192,128]{2,1,0:T(8,128)(2,1)}), bf16[1,1024,128]{2,1,0:T(8,128)(2,1)}) %reduce-scatter.5.cloned.1.call-update) | async-done | bytes 262160 | tf_op jit(solution)/shard_map/reduce_scatter | solution.py:109
  654.5 34.9 %reduce-scatter.7.cloned.1.call-done = bf16[1,1024,128]{2,1,0:T(8,128)(2,1)} async-done(((bf16[1,8192,128]{2,1,0:T(8,128)(2,1)}), bf16[1,1024,128]{2,1,0:T(8,128)(2,1)}) %reduce-scatter.7.cloned.1.call-update) | async-done | bytes 262160 | tf_op jit(solution)/shard_map/reduce_scatter | solution.py:112
  691.2 35.0 %reduce-scatter.9.cloned.1.call-done = bf16[1,1024,128]{2,1,0:T(8,128)(2,1)} async-done(((bf16[1,8192,128]{2,1,0:T(8,128)(2,1)}), bf16[1,1024,128]{2,1,0:T(8,128)(2,1)}) %reduce-scatter.9.cloned.1.call-update) | async-done | bytes 262160 | tf_op jit(solution)/shard_map/reduce_scatter | solution.py:115
  727.9 35.0 %reduce-scatter.11.cloned.1.call-done = bf16[1,1024,128]{2,1,0:T(8,128)(2,1)} async-done(((bf16[1,8192,128]{2,1,0:T(8,128)(2,1)}), bf16[1,1024,128]{2,1,0:T(8,128)(2,1)}) %reduce-scatter.11.cloned.1.call-update) | async-done | bytes 262160 | tf_op jit(solution)/shard_map/reduce_scatter | solution.py:118
  (340 shorter events, 364.8 us)
Async XLA Ops:
  7.2 126.4 %copy-start.10 = (s32[1,4,32]{2,1,0:T(4,128)S(1)}, s32[1,4,32]{2,1,0:T(4,128)}, u32[]{:S(2)}) copy-start(s32[1,4,32]{2,1,0:T(4,128)} %param.16) | copy-start | bytes 1540
  7.2 34.3 %all-gather.5.cloned.1.call-start = ((), (), s32[]{:S(2)}) async-start(), calls=%async_computation.4 | async-start | bytes 2359296 | tf_op jit(solution)/shard_map/all_gather | solution.py:37
  7.9 63.8 %all-gather.7.cloned.1.call-start = ((), (), s32[]{:S(2)}) async-start(), calls=%async_computation.5 | async-start | bytes 2359296 | tf_op jit(solution)/shard_map/all_gather | solution.py:38
  8.7 93.2 %all-gather.9.cloned.1.call-start = ((), (), s32[]{:S(2)}) async-start(), calls=%async_computation.6 | async-start | bytes 2359296 | tf_op jit(solution)/shard_map/all_gather | solution.py:39
  9.4 122.6 %all-gather.11.cloned.1.call-start = ((), (), s32[]{:S(2)}) async-start(), calls=%async_computation.7 | async-start | bytes 2359296 | tf_op jit(solution)/shard_map/all_gather | solution.py:40
  10.0 642.8 %reduce-scatter.5.cloned.1.call-start = ((), (), s32[]{:S(2)}) async-start(), calls=%async_computation.8 | async-start | bytes 2359296 | tf_op jit(solution)/shard_map/reduce_scatter | solution.py:109
  41.4 92.1 %copy-start = (bf16[1,8192,128]{2,1,0:T(8,128)(2,1)S(1)}, bf16[1,8192,128]{2,1,0:T(8,128)(2,1)}, u32[]{:S(2)}) copy-start(bf16[1,8192,128]{2,1,0:T(8,128)(2,1)} %all-gather.5.cloned.1.call-done) | copy-start | bytes 6291460
  145.3 13.4 %collective-permute-start = (bf16[32,8192]{1,0:T(8,128)(2,1)}, bf16[32,8192]{1,0:T(8,128)(2,1)S(1)}, u32[]{:S(2)}, u32[]{:S(2)}) collective-permute-start(bf16[32,8192]{1,0:T(8,128)(2,1)} %copy-done.9), channel_id=1, source_target_pairs={{0,8},{8,16},{16,24},{1,9},{9,17},{17,25},{2,10},{10,18},{18,26},{... | collective-permute-start | bytes 1572872 | tf_op jit(solution)/shard_map/while/body/eval_jaxpr/ppermute | solution.py:10
  170.4 15.7 %collective-permute-start = (bf16[32,8192]{1,0:T(8,128)(2,1)}, bf16[32,8192]{1,0:T(8,128)(2,1)S(1)}, u32[]{:S(2)}, u32[]{:S(2)}) collective-permute-start(bf16[32,8192]{1,0:T(8,128)(2,1)} %copy-done.9), channel_id=1, source_target_pairs={{0,8},{8,16},{16,24},{1,9},{9,17},{17,25},{2,10},{10,18},{18,26},{... | collective-permute-start | bytes 1572872 | tf_op jit(solution)/shard_map/while/body/eval_jaxpr/ppermute | solution.py:10
  197.8 14.7 %collective-permute-start = (bf16[32,8192]{1,0:T(8,128)(2,1)}, bf16[32,8192]{1,0:T(8,128)(2,1)S(1)}, u32[]{:S(2)}, u32[]{:S(2)}) collective-permute-start(bf16[32,8192]{1,0:T(8,128)(2,1)} %copy-done.9), channel_id=1, source_target_pairs={{0,8},{8,16},{16,24},{1,9},{9,17},{17,25},{2,10},{10,18},{18,26},{... | collective-permute-start | bytes 1572872 | tf_op jit(solution)/shard_map/while/body/eval_jaxpr/ppermute | solution.py:10
  224.3 13.8 %collective-permute-start = (bf16[32,8192]{1,0:T(8,128)(2,1)}, bf16[32,8192]{1,0:T(8,128)(2,1)S(1)}, u32[]{:S(2)}, u32[]{:S(2)}) collective-permute-start(bf16[32,8192]{1,0:T(8,128)(2,1)} %copy-done.9), channel_id=1, source_target_pairs={{0,8},{8,16},{16,24},{1,9},{9,17},{17,25},{2,10},{10,18},{18,26},{... | collective-permute-start | bytes 1572872 | tf_op jit(solution)/shard_map/while/body/eval_jaxpr/ppermute | solution.py:10
  242.1 21.3 %collective-permute-start = (bf16[32,8192]{1,0:T(8,128)(2,1)}, bf16[32,8192]{1,0:T(8,128)(2,1)S(1)}, u32[]{:S(2)}, u32[]{:S(2)}) collective-permute-start(bf16[32,8192]{1,0:T(8,128)(2,1)} %copy-done.9), channel_id=1, source_target_pairs={{0,8},{8,16},{16,24},{1,9},{9,17},{17,25},{2,10},{10,18},{18,26},{... | collective-permute-start | bytes 1572872 | tf_op jit(solution)/shard_map/while/body/eval_jaxpr/ppermute | solution.py:10
  267.5 13.2 %collective-permute-start = (bf16[32,8192]{1,0:T(8,128)(2,1)}, bf16[32,8192]{1,0:T(8,128)(2,1)S(1)}, u32[]{:S(2)}, u32[]{:S(2)}) collective-permute-start(bf16[32,8192]{1,0:T(8,128)(2,1)} %copy-done.9), channel_id=1, source_target_pairs={{0,8},{8,16},{16,24},{1,9},{9,17},{17,25},{2,10},{10,18},{18,26},{... | collective-permute-start | bytes 1572872 | tf_op jit(solution)/shard_map/while/body/eval_jaxpr/ppermute | solution.py:10
  284.7 20.0 %collective-permute-start = (bf16[32,8192]{1,0:T(8,128)(2,1)}, bf16[32,8192]{1,0:T(8,128)(2,1)S(1)}, u32[]{:S(2)}, u32[]{:S(2)}) collective-permute-start(bf16[32,8192]{1,0:T(8,128)(2,1)} %copy-done.9), channel_id=1, source_target_pairs={{0,8},{8,16},{16,24},{1,9},{9,17},{17,25},{2,10},{10,18},{18,26},{... | collective-permute-start | bytes 1572872 | tf_op jit(solution)/shard_map/while/body/eval_jaxpr/ppermute | solution.py:10
  315.9 18.3 %collective-permute-start.1 = (bf16[32,8192]{1,0:T(8,128)(2,1)S(1)}, bf16[32,8192]{1,0:T(8,128)(2,1)S(1)}, u32[]{:S(2)}, u32[]{:S(2)}) collective-permute-start(bf16[32,8192]{1,0:T(8,128)(2,1)S(1)} %get-tuple-element.1017), channel_id=1, source_target_pairs={{8,0},{16,8},{24,16},{9,1},{17,9},{25,17},{10,2},{18,10},{26,18},{... | collective-permute-start | bytes 1572872 | tf_op jit(solution)/shard_map/while/body/eval_jaxpr/ppermute | solution.py:10
  344.0 23.1 %collective-permute-start.1 = (bf16[32,8192]{1,0:T(8,128)(2,1)S(1)}, bf16[32,8192]{1,0:T(8,128)(2,1)S(1)}, u32[]{:S(2)}, u32[]{:S(2)}) collective-permute-start(bf16[32,8192]{1,0:T(8,128)(2,1)S(1)} %get-tuple-element.1017), channel_id=1, source_target_pairs={{8,0},{16,8},{24,16},{9,1},{17,9},{25,17},{10,2},{18,10},{26,18},{... | collective-permute-start | bytes 1572872 | tf_op jit(solution)/shard_map/while/body/eval_jaxpr/ppermute | solution.py:10
  376.9 42.3 %collective-permute-start.1 = (bf16[32,8192]{1,0:T(8,128)(2,1)S(1)}, bf16[32,8192]{1,0:T(8,128)(2,1)S(1)}, u32[]{:S(2)}, u32[]{:S(2)}) collective-permute-start(bf16[32,8192]{1,0:T(8,128)(2,1)S(1)} %get-tuple-element.1017), channel_id=1, source_target_pairs={{8,0},{16,8},{24,16},{9,1},{17,9},{25,17},{10,2},{18,10},{26,18},{... | collective-permute-start | bytes 1572872 | tf_op jit(solution)/shard_map/while/body/eval_jaxpr/ppermute | solution.py:10
  420.0 3.8 copy-start.4
  436.2 4.0 copy-start.1
  443.7 23.7 %collective-permute-start.1 = (bf16[32,8192]{1,0:T(8,128)(2,1)S(1)}, bf16[32,8192]{1,0:T(8,128)(2,1)S(1)}, u32[]{:S(2)}, u32[]{:S(2)}) collective-permute-start(bf16[32,8192]{1,0:T(8,128)(2,1)S(1)} %get-tuple-element.1017), channel_id=1, source_target_pairs={{8,0},{16,8},{24,16},{9,1},{17,9},{25,17},{10,2},{18,10},{26,18},{... | collective-permute-start | bytes 1572872 | tf_op jit(solution)/shard_map/while/body/eval_jaxpr/ppermute | solution.py:10
  468.2 3.8 copy-start.4
  484.4 4.0 copy-start.1
  491.9 23.7 %collective-permute-start.1 = (bf16[32,8192]{1,0:T(8,128)(2,1)S(1)}, bf16[32,8192]{1,0:T(8,128)(2,1)S(1)}, u32[]{:S(2)}, u32[]{:S(2)}) collective-permute-start(bf16[32,8192]{1,0:T(8,128)(2,1)S(1)} %get-tuple-element.1017), channel_id=1, source_target_pairs={{8,0},{16,8},{24,16},{9,1},{17,9},{25,17},{10,2},{18,10},{26,18},{... | collective-permute-start | bytes 1572872 | tf_op jit(solution)/shard_map/while/body/eval_jaxpr/ppermute | solution.py:10
  516.5 3.8 copy-start.4
  532.6 4.0 copy-start.1
  540.1 23.7 %collective-permute-start.1 = (bf16[32,8192]{1,0:T(8,128)(2,1)S(1)}, bf16[32,8192]{1,0:T(8,128)(2,1)S(1)}, u32[]{:S(2)}, u32[]{:S(2)}) collective-permute-start(bf16[32,8192]{1,0:T(8,128)(2,1)S(1)} %get-tuple-element.1017), channel_id=1, source_target_pairs={{8,0},{16,8},{24,16},{9,1},{17,9},{25,17},{10,2},{18,10},{26,18},{... | collective-permute-start | bytes 1572872 | tf_op jit(solution)/shard_map/while/body/eval_jaxpr/ppermute | solution.py:10
  564.7 3.8 copy-start.4
  580.8 4.0 copy-start.1
  588.4 23.1 %collective-permute-start.1 = (bf16[32,8192]{1,0:T(8,128)(2,1)S(1)}, bf16[32,8192]{1,0:T(8,128)(2,1)S(1)}, u32[]{:S(2)}, u32[]{:S(2)}) collective-permute-start(bf16[32,8192]{1,0:T(8,128)(2,1)S(1)} %get-tuple-element.1017), channel_id=1, source_target_pairs={{8,0},{16,8},{24,16},{9,1},{17,9},{25,17},{10,2},{18,10},{26,18},{... | collective-permute-start | bytes 1572872 | tf_op jit(solution)/shard_map/while/body/eval_jaxpr/ppermute | solution.py:10
  616.0 73.4 %reduce-scatter.7.cloned.1.call-start = ((), (), s32[]{:S(2)}) async-start(), calls=%async_computation.9 | async-start | bytes 2359296 | tf_op jit(solution)/shard_map/reduce_scatter | solution.py:112
  619.8 106.3 %reduce-scatter.9.cloned.1.call-start = ((), (), s32[]{:S(2)}) async-start(), calls=%async_computation.10 | async-start | bytes 2359296 | tf_op jit(solution)/shard_map/reduce_scatter | solution.py:115
  623.6 139.3 %reduce-scatter.11.cloned.1.call-start = ((), (), s32[]{:S(2)}) async-start(), calls=%async_computation.11 | async-start | bytes 2359296 | tf_op jit(solution)/shard_map/reduce_scatter | solution.py:118
  (34 other events, 51.2 us)
Sparse Core Ops, SparseCore 0:
  9.6 31.7 all-gather.4
  43.0 28.5 all-gather.6
  73.3 28.5 all-gather.8
  103.4 28.5 all-gather.10
  616.1 36.5 reduce-scatter.4
  654.9 34.4 reduce-scatter.6
  691.7 34.4 reduce-scatter.8
  728.4 34.4 reduce-scatter.10
where the time goes:
time: 774 us; the launch traced here: 772 us
  waiting for transfers between devices  343 us (44%)
  other arithmetic  191 us (25%)
  matrix products  108 us (14%)
  local copies, waits for them, and re-layouts  59.5 us (8%)
  starting transfers between devices  54.1 us (7%)
  between operations  14.2 us (2%)
    add x14, other arithmetic, backward_tick(): totals = tuple((total + part for total, part in zip(totals, parts)))  134 us
    ppermute x14, waiting for transfers between devices, shifted(): return lax.ppermute(block, axis, route)  88.6 us
    ppermute x14, starting transfers between devices, shifted(): return lax.ppermute(block, axis, route)  53.8 us
    reduce_scatter x1, waiting for transfers between devices, shards(): lax.psum_scatter(totals[3].astype(jnp.bfloat16)[None], 'dp', scatter_dime...  35 us
    reduce_scatter x1, waiting for transfers between devices, shards(): lax.psum_scatter(totals[2].astype(jnp.bfloat16)[None], 'dp', scatter_dime...  35 us
    reduce_scatter x1, waiting for transfers between devices, shards(): lax.psum_scatter(totals[1].astype(jnp.bfloat16)[None], 'dp', scatter_dime...  34.9 us
    dot_general x16, matrix products, section(): jnp.dot(normed, w_key, preferred_element_type=jnp.float32)  32.3 us
    all_gather x1, waiting for transfers between devices, shards(): lax.all_gather(w_query, 'dp', axis=1, tiled=True)  31.4 us
  transfers between devices with their start and end apart: 22, of which 19 were waited for; matrix products, arithmetic and copies ran while one was open for 21% of the time, Pallas kernels for 0%

commit v1 on v0

--- a/solution.py
+++ b/solution.py
@@ -2,6 +2,27 @@
 import jax.numpy as jnp
 from jax import lax
 from jax.sharding import PartitionSpec as P
+
+
+def gather_around(shard, axis, dim):
+    count, mine, width = (lax.axis_size(axis), lax.axis_index(axis), shard.shape[dim])
+    forward = [(i, (i + 1) % count) for i in range(count)]
+    downward = [(i, (i - 1) % count) for i in range(count)]
+    whole = jnp.zeros((*shard.shape[:dim], count * width, *shard.shape[dim + 1 :]), shard.dtype)
+    whole = lax.dynamic_update_slice_in_dim(whole, shard, mine * width, axis=dim)
+    from_left = from_right = shard
+    middle = count // 2
+    for step in range(1, middle + 1):
+        from_left = lax.ppermute(from_left, axis, forward)
+        whole = lax.dynamic_update_slice_in_dim(
+            whole, from_left, (mine - step) % count * width, axis=dim
+        )
+        if step < count - middle:
+            from_right = lax.ppermute(from_right, axis, downward)
+            whole = lax.dynamic_update_slice_in_dim(
+                whole, from_right, (mine + step) % count * width, axis=dim
+            )
+    return whole
 
 
 def shifted(block, axis, distance):
@@ -37,7 +58,7 @@
         lax.all_gather(w_query, "dp", axis=1, tiled=True),
         lax.all_gather(w_key, "dp", axis=1, tiled=True),
         lax.all_gather(w_value, "dp", axis=1, tiled=True),
-        lax.all_gather(w_out, "dp", axis=1, tiled=True),
+        gather_around(w_out, "dp", 1),
     )
     layer = (full_query[0], full_key[0], full_value[0], full_out[0])
     features = inputs[0]

time: 774 us -> 762 us (0.984)
  waiting for transfers between devices: 343 us -> 306 us
  starting transfers between devices: 54.1 us -> 66.1 us
    all_gather x1, waiting for transfers between devices: 31.4 us -> 0.01 us  [shards(): lax.all_gather(w_query, 'dp', axis=1, tiled=True)]
    all_gather x1 -> x0, waiting for transfers between devices: 30.1 us -> none  [shards(): lax.all_gather(w_out, 'dp', axis=1, tiled=True)]
    ppermute x0 -> x7, waiting for transfers between devices: none -> 26 us  [the longest x4 17.8 us: gather_around(): from_left = lax.ppermute(from_left, axis, forward)]
    ppermute x0 -> x7, starting transfers between devices: none -> 12.1 us  [the longest x3 11.6 us: gather_around(): from_right = lax.ppermute(from_right, axis, downward)]
  transfers between devices with their start and end apart: 22 -> 28, of which waited for: 19 -> 24; matrix products, arithmetic and copies ran while one was open for 21% -> 23% of each run, Pallas kernels for 0% -> 0%
where the time goes in v1:
time: 762 us; the launch traced here: 759 us
  waiting for transfers between devices  306 us (40%)
  other arithmetic  190 us (25%)
  matrix products  115 us (15%)
  local copies, waits for them, and re-layouts  66.8 us (9%)
  starting transfers between devices  66.1 us (9%)
  between operations  14.2 us (2%)
    add x14, other arithmetic, backward_tick(): totals = tuple((total + part for total, part in zip(totals, parts)))  134 us
    ppermute x14, waiting for transfers between devices, shifted(): return lax.ppermute(block, axis, route)  92.9 us
    ppermute x14, starting transfers between devices, shifted(): return lax.ppermute(block, axis, route)  53.7 us
    reduce_scatter x1, waiting for transfers between devices, shards(): lax.psum_scatter(totals[3].astype(jnp.bfloat16)[None], 'dp', scatter_dime...  35 us
    reduce_scatter x1, waiting for transfers between devices, shards(): lax.psum_scatter(totals[1].astype(jnp.bfloat16)[None], 'dp', scatter_dime...  34.7 us
    reduce_scatter x1, waiting for transfers between devices, shards(): lax.psum_scatter(totals[2].astype(jnp.bfloat16)[None], 'dp', scatter_dime...  34.6 us
    dot_general x16, matrix products, section(): jnp.dot(normed, w_key, preferred_element_type=jnp.float32)  32.3 us
    another operation x22, local copies, waits for them, and re-layouts  30.8 us
  transfers between devices with their start and end apart: 28, of which 24 were waited for; matrix products, arithmetic and copies ran while one was open for 23% of the time, Pallas kernels for 0%

profile of v1, /device:TPU:0, one launch (start us, length us, event | category | flops | bytes accessed | tf_op | source)
XLA Modules:
  0.0 759.4 jit_solution(10322608445339710844)
XLA Ops:
  54.9 26.2 %all-gather.6.cloned.1.call-done = bf16[1,8192,128]{2,1,0:T(8,128)(2,1)} async-done(((bf16[1,1024,128]{2,1,0:T(8,128)(2,1)}), bf16[1,8192,128]{2,1,0:T(8,128)(2,1)}) %all-gather.6.cloned.1.call-update) | async-done | bytes 2097168 | tf_op jit(solution)/shard_map/all_gather | solution.py:59
  81.1 30.2 %all-gather.8.cloned.1.call-done = bf16[1,8192,128]{2,1,0:T(8,128)(2,1)} async-done(((bf16[1,1024,128]{2,1,0:T(8,128)(2,1)}), bf16[1,8192,128]{2,1,0:T(8,128)(2,1)}) %all-gather.8.cloned.1.call-update) | async-done | bytes 2097168 | tf_op jit(solution)/shard_map/all_gather | solution.py:60
  112.9 170.8 %while.42 = (s32[]{:T(128)}, bf16[32,8192]{1,0:T(8,128)(2,1)S(1)}, bf16[4,32,8192]{2,1,0:T(8,128)(2,1)}, s32[]{:T(128)}, pred[]{:T(512)}, /*index=5*/bf16[4,32,8...) while((s32[]{:T(128)}, bf16[32,8192]{1,0:T(8,128)(2,1)S(1)}, ...), condition=%wide.region_6.7_spmd, body=%wide.region_0.6_spmd.sunk | while | flops 273452000 | bytes 19447128 | solution.py:91
  125.9 12.1 %collective-permute-done = bf16[32,8192]{1,0:T(8,128)(2,1)S(1)} collective-permute-done((bf16[32,8192]{1,0:T(8,128)(2,1)}, bf16[32,8192]{1,0:T(8,128)(2,1)S(1)}, u32[]{:S(2)}, u32[]{:S(2)}) %collective-permute-start) | collective-permute-done | bytes 524320 | tf_op jit(solution)/shard_map/while/body/eval_jaxpr/ppermute | solution.py:31
  154.0 11.3 %collective-permute-done = bf16[32,8192]{1,0:T(8,128)(2,1)S(1)} collective-permute-done((bf16[32,8192]{1,0:T(8,128)(2,1)}, bf16[32,8192]{1,0:T(8,128)(2,1)S(1)}, u32[]{:S(2)}, u32[]{:S(2)}) %collective-permute-start) | collective-permute-done | bytes 524320 | tf_op jit(solution)/shard_map/while/body/eval_jaxpr/ppermute | solution.py:31
  181.4 10.4 %collective-permute-done = bf16[32,8192]{1,0:T(8,128)(2,1)S(1)} collective-permute-done((bf16[32,8192]{1,0:T(8,128)(2,1)}, bf16[32,8192]{1,0:T(8,128)(2,1)S(1)}, u32[]{:S(2)}, u32[]{:S(2)}) %collective-permute-start) | collective-permute-done | bytes 524320 | tf_op jit(solution)/shard_map/while/body/eval_jaxpr/ppermute | solution.py:31
  207.8 9.5 %collective-permute-done = bf16[32,8192]{1,0:T(8,128)(2,1)S(1)} collective-permute-done((bf16[32,8192]{1,0:T(8,128)(2,1)}, bf16[32,8192]{1,0:T(8,128)(2,1)S(1)}, u32[]{:S(2)}, u32[]{:S(2)}) %collective-permute-start) | collective-permute-done | bytes 524320 | tf_op jit(solution)/shard_map/while/body/eval_jaxpr/ppermute | solution.py:31
  221.3 12.4 %collective-permute-start = (bf16[32,8192]{1,0:T(8,128)(2,1)}, bf16[32,8192]{1,0:T(8,128)(2,1)S(1)}, u32[]{:S(2)}, u32[]{:S(2)}) collective-permute-start(bf16[32,8192]{1,0:T(8,128)(2,1)} %copy-done.8), channel_id=1, source_target_pairs={{0,8},{8,16},{16,24},{1,9},{9,17},{17,25},{2,10},{10,18},{18,26},{... | collective-permute-start | bytes 1572872 | tf_op jit(solution)/shard_map/while/body/eval_jaxpr/ppermute | solution.py:31
  263.7 12.9 %collective-permute-start = (bf16[32,8192]{1,0:T(8,128)(2,1)}, bf16[32,8192]{1,0:T(8,128)(2,1)S(1)}, u32[]{:S(2)}, u32[]{:S(2)}) collective-permute-start(bf16[32,8192]{1,0:T(8,128)(2,1)} %copy-done.8), channel_id=1, source_target_pairs={{0,8},{8,16},{16,24},{1,9},{9,17},{17,25},{2,10},{10,18},{18,26},{... | collective-permute-start | bytes 1572872 | tf_op jit(solution)/shard_map/while/body/eval_jaxpr/ppermute | solution.py:31
  286.1 315.4 %while.43 = (s32[]{:T(128)}, bf16[32,8192]{1,0:T(8,128)(2,1)}, f32[8192,128]{1,0:T(8,128)}, f32[8192,128]{1,0:T(8,128)}, f32[8192,128]{1,0:T(8,128)}, /*index=5*...) while((s32[]{:T(128)}, bf16[32,8192]{1,0:T(8,128)(2,1)}, ...), condition=%wide.region_17.18_spmd.clone, body=%wide.region_7.17_spmd.clone.sunk | while | flops 767129792 | bytes 145457920 | solution.py:126
  286.1 8.9 %conditional.6 = (bf16[32,8192]{1,0:T(8,128)(2,1)S(1)}, f32[8192,128]{1,0:T(8,128)}, f32[8192,128]{1,0:T(8,128)}, f32[8192,128]{1,0:T(8,128)}, f32[8192,128]{1,0:T(8,128)}) conditional(s32[]{:T(128)} %convert_element_type.326, () %tuple.115, (pred[]{:T(512)}, bf16[4,32,8192]{2,1,0:T(8,128)(2,1)}, s32[]{:T(128)}, bf16[32,8192]{1,0:T(8,128)(2,1)}, ...), branch_computations={%region_8.8_spmd, %region_9.16_spmd} | conditional | flops 758479040 | bytes 88309608 | solution.py:116
  325.5 9.9 %select_add_fusion.7 = (f32[8192,128]{1,0:T(8,128)}, f32[8192,128]{1,0:T(8,128)}) fusion(f32[8192,128]{1,0:T(8,128)} %get-tuple-element.1022, f32[8192,128]{1,0:T(8,128)} %get-tuple-element.1106, pred[]{:T(512)S(6)} %compare.10, f32[8192,128]{1,0:T(8,128)} %get-tuple-element.1023, f32[8192,128]{1,0:T(8,128)} %get-tuple-element.1105), kind=kLoop, calls=%fused_computation.93.clone.1 | loop fusion | flops 4194304 | bytes 25165824 | tf_op jit(solution)/shard_map/while/body/eval_jaxpr/add | solution.py:117
  335.4 9.9 %select_add_fusion.6 = (f32[8192,128]{1,0:T(8,128)}, f32[8192,128]{1,0:T(8,128)}) fusion(f32[8192,128]{1,0:T(8,128)} %get-tuple-element.1018, f32[8192,128]{1,0:T(8,128)} %get-tuple-element.1104, pred[]{:T(512)S(6)} %compare.10, f32[8192,128]{1,0:T(8,128)} %get-tuple-element.1019, f32[8192,128]{1,0:T(8,128)} %get-tuple-element.1103), kind=kLoop, calls=%fused_computation.95.clone.1 | loop fusion | flops 4194304 | bytes 25165824 | tf_op jit(solution)/shard_map/while/body/eval_jaxpr/add | solution.py:117
  358.3 9.9 %select_add_fusion.7 = (f32[8192,128]{1,0:T(8,128)}, f32[8192,128]{1,0:T(8,128)}) fusion(f32[8192,128]{1,0:T(8,128)} %get-tuple-element.1022, f32[8192,128]{1,0:T(8,128)} %get-tuple-element.1106, pred[]{:T(512)S(6)} %compare.10, f32[8192,128]{1,0:T(8,128)} %get-tuple-element.1023, f32[8192,128]{1,0:T(8,128)} %get-tuple-element.1105), kind=kLoop, calls=%fused_computation.93.clone.1 | loop fusion | flops 4194304 | bytes 25165824 | tf_op jit(solution)/shard_map/while/body/eval_jaxpr/add | solution.py:117
  368.2 9.9 %select_add_fusion.6 = (f32[8192,128]{1,0:T(8,128)}, f32[8192,128]{1,0:T(8,128)}) fusion(f32[8192,128]{1,0:T(8,128)} %get-tuple-element.1018, f32[8192,128]{1,0:T(8,128)} %get-tuple-element.1104, pred[]{:T(512)S(6)} %compare.10, f32[8192,128]{1,0:T(8,128)} %get-tuple-element.1019, f32[8192,128]{1,0:T(8,128)} %get-tuple-element.1103), kind=kLoop, calls=%fused_computation.95.clone.1 | loop fusion | flops 4194304 | bytes 25165824 | tf_op jit(solution)/shard_map/while/body/eval_jaxpr/add | solution.py:117
  379.0 23.6 %collective-permute-done.1 = bf16[32,8192]{1,0:T(8,128)(2,1)S(1)} collective-permute-done((bf16[32,8192]{1,0:T(8,128)(2,1)S(1)}, bf16[32,8192]{1,0:T(8,128)(2,1)S(1)}, u32[]{:S(2)}, u32[]{:S(2)}) %collective-permute-start.1) | collective-permute-done | bytes 524320 | tf_op jit(solution)/shard_map/while/body/eval_jaxpr/ppermute | solution.py:31
  403.4 25.1 %conditional.6 = (bf16[32,8192]{1,0:T(8,128)(2,1)S(1)}, f32[8192,128]{1,0:T(8,128)}, f32[8192,128]{1,0:T(8,128)}, f32[8192,128]{1,0:T(8,128)}, f32[8192,128]{1,0:T(8,128)}) conditional(s32[]{:T(128)} %convert_element_type.326, () %tuple.115, (pred[]{:T(512)}, bf16[4,32,8192]{2,1,0:T(8,128)(2,1)}, s32[]{:T(128)}, bf16[32,8192]{1,0:T(8,128)(2,1)}, ...), branch_computations={%region_8.8_spmd, %region_9.16_spmd} | conditional | flops 758479040 | bytes 88309608 | solution.py:116
  430.9 9.9 %select_add_fusion.7 = (f32[8192,128]{1,0:T(8,128)}, f32[8192,128]{1,0:T(8,128)}) fusion(f32[8192,128]{1,0:T(8,128)} %get-tuple-element.1022, f32[8192,128]{1,0:T(8,128)} %get-tuple-element.1106, pred[]{:T(512)S(6)} %compare.10, f32[8192,128]{1,0:T(8,128)} %get-tuple-element.1023, f32[8192,128]{1,0:T(8,128)} %get-tuple-element.1105), kind=kLoop, calls=%fused_computation.93.clone.1 | loop fusion | flops 4194304 | bytes 25165824 | tf_op jit(solution)/shard_map/while/body/eval_jaxpr/add | solution.py:117
  440.9 9.9 %select_add_fusion.6 = (f32[8192,128]{1,0:T(8,128)}, f32[8192,128]{1,0:T(8,128)}) fusion(f32[8192,128]{1,0:T(8,128)} %get-tuple-element.1018, f32[8192,128]{1,0:T(8,128)} %get-tuple-element.1104, pred[]{:T(512)S(6)} %compare.10, f32[8192,128]{1,0:T(8,128)} %get-tuple-element.1019, f32[8192,128]{1,0:T(8,128)} %get-tuple-element.1103), kind=kLoop, calls=%fused_computation.95.clone.1 | loop fusion | flops 4194304 | bytes 25165824 | tf_op jit(solution)/shard_map/while/body/eval_jaxpr/add | solution.py:117
  453.1 25.1 %conditional.6 = (bf16[32,8192]{1,0:T(8,128)(2,1)S(1)}, f32[8192,128]{1,0:T(8,128)}, f32[8192,128]{1,0:T(8,128)}, f32[8192,128]{1,0:T(8,128)}, f32[8192,128]{1,0:T(8,128)}) conditional(s32[]{:T(128)} %convert_element_type.326, () %tuple.115, (pred[]{:T(512)}, bf16[4,32,8192]{2,1,0:T(8,128)(2,1)}, s32[]{:T(128)}, bf16[32,8192]{1,0:T(8,128)(2,1)}, ...), branch_computations={%region_8.8_spmd, %region_9.16_spmd} | conditional | flops 758479040 | bytes 88309608 | solution.py:116
  480.6 9.9 %select_add_fusion.7 = (f32[8192,128]{1,0:T(8,128)}, f32[8192,128]{1,0:T(8,128)}) fusion(f32[8192,128]{1,0:T(8,128)} %get-tuple-element.1022, f32[8192,128]{1,0:T(8,128)} %get-tuple-element.1106, pred[]{:T(512)S(6)} %compare.10, f32[8192,128]{1,0:T(8,128)} %get-tuple-element.1023, f32[8192,128]{1,0:T(8,128)} %get-tuple-element.1105), kind=kLoop, calls=%fused_computation.93.clone.1 | loop fusion | flops 4194304 | bytes 25165824 | tf_op jit(solution)/shard_map/while/body/eval_jaxpr/add | solution.py:117
  490.5 9.9 %select_add_fusion.6 = (f32[8192,128]{1,0:T(8,128)}, f32[8192,128]{1,0:T(8,128)}) fusion(f32[8192,128]{1,0:T(8,128)} %get-tuple-element.1018, f32[8192,128]{1,0:T(8,128)} %get-tuple-element.1104, pred[]{:T(512)S(6)} %compare.10, f32[8192,128]{1,0:T(8,128)} %get-tuple-element.1019, f32[8192,128]{1,0:T(8,128)} %get-tuple-element.1103), kind=kLoop, calls=%fused_computation.95.clone.1 | loop fusion | flops 4194304 | bytes 25165824 | tf_op jit(solution)/shard_map/while/body/eval_jaxpr/add | solution.py:117
  502.8 25.1 %conditional.6 = (bf16[32,8192]{1,0:T(8,128)(2,1)S(1)}, f32[8192,128]{1,0:T(8,128)}, f32[8192,128]{1,0:T(8,128)}, f32[8192,128]{1,0:T(8,128)}, f32[8192,128]{1,0:T(8,128)}) conditional(s32[]{:T(128)} %convert_element_type.326, () %tuple.115, (pred[]{:T(512)}, bf16[4,32,8192]{2,1,0:T(8,128)(2,1)}, s32[]{:T(128)}, bf16[32,8192]{1,0:T(8,128)(2,1)}, ...), branch_computations={%region_8.8_spmd, %region_9.16_spmd} | conditional | flops 758479040 | bytes 88309608 | solution.py:116
  530.3 9.9 %select_add_fusion.7 = (f32[8192,128]{1,0:T(8,128)}, f32[8192,128]{1,0:T(8,128)}) fusion(f32[8192,128]{1,0:T(8,128)} %get-tuple-element.1022, f32[8192,128]{1,0:T(8,128)} %get-tuple-element.1106, pred[]{:T(512)S(6)} %compare.10, f32[8192,128]{1,0:T(8,128)} %get-tuple-element.1023, f32[8192,128]{1,0:T(8,128)} %get-tuple-element.1105), kind=kLoop, calls=%fused_computation.93.clone.1 | loop fusion | flops 4194304 | bytes 25165824 | tf_op jit(solution)/shard_map/while/body/eval_jaxpr/add | solution.py:117
  540.2 9.9 %select_add_fusion.6 = (f32[8192,128]{1,0:T(8,128)}, f32[8192,128]{1,0:T(8,128)}) fusion(f32[8192,128]{1,0:T(8,128)} %get-tuple-element.1018, f32[8192,128]{1,0:T(8,128)} %get-tuple-element.1104, pred[]{:T(512)S(6)} %compare.10, f32[8192,128]{1,0:T(8,128)} %get-tuple-element.1019, f32[8192,128]{1,0:T(8,128)} %get-tuple-element.1103), kind=kLoop, calls=%fused_computation.95.clone.1 | loop fusion | flops 4194304 | bytes 25165824 | tf_op jit(solution)/shard_map/while/body/eval_jaxpr/add | solution.py:117
  552.4 25.1 %conditional.6 = (bf16[32,8192]{1,0:T(8,128)(2,1)S(1)}, f32[8192,128]{1,0:T(8,128)}, f32[8192,128]{1,0:T(8,128)}, f32[8192,128]{1,0:T(8,128)}, f32[8192,128]{1,0:T(8,128)}) conditional(s32[]{:T(128)} %convert_element_type.326, () %tuple.115, (pred[]{:T(512)}, bf16[4,32,8192]{2,1,0:T(8,128)(2,1)}, s32[]{:T(128)}, bf16[32,8192]{1,0:T(8,128)(2,1)}, ...), branch_computations={%region_8.8_spmd, %region_9.16_spmd} | conditional | flops 758479040 | bytes 88309608 | solution.py:116
  579.9 9.9 %select_add_fusion.7 = (f32[8192,128]{1,0:T(8,128)}, f32[8192,128]{1,0:T(8,128)}) fusion(f32[8192,128]{1,0:T(8,128)} %get-tuple-element.1022, f32[8192,128]{1,0:T(8,128)} %get-tuple-element.1106, pred[]{:T(512)S(6)} %compare.10, f32[8192,128]{1,0:T(8,128)} %get-tuple-element.1023, f32[8192,128]{1,0:T(8,128)} %get-tuple-element.1105), kind=kLoop, calls=%fused_computation.93.clone.1 | loop fusion | flops 4194304 | bytes 25165824 | tf_op jit(solution)/shard_map/while/body/eval_jaxpr/add | solution.py:117
  589.9 9.9 %select_add_fusion.6 = (f32[8192,128]{1,0:T(8,128)}, f32[8192,128]{1,0:T(8,128)}) fusion(f32[8192,128]{1,0:T(8,128)} %get-tuple-element.1018, f32[8192,128]{1,0:T(8,128)} %get-tuple-element.1104, pred[]{:T(512)S(6)} %compare.10, f32[8192,128]{1,0:T(8,128)} %get-tuple-element.1019, f32[8192,128]{1,0:T(8,128)} %get-tuple-element.1103), kind=kLoop, calls=%fused_computation.95.clone.1 | loop fusion | flops 4194304 | bytes 25165824 | tf_op jit(solution)/shard_map/while/body/eval_jaxpr/add | solution.py:117
  616.6 24.6 %reduce-scatter.5.cloned.1.call-done = bf16[1,1024,128]{2,1,0:T(8,128)(2,1)} async-done(((bf16[1,8192,128]{2,1,0:T(8,128)(2,1)}), bf16[1,1024,128]{2,1,0:T(8,128)(2,1)}) %reduce-scatter.5.cloned.1.call-update) | async-done | bytes 262160 | tf_op jit(solution)/shard_map/reduce_scatter | solution.py:130
  643.0 34.7 %reduce-scatter.7.cloned.1.call-done = bf16[1,1024,128]{2,1,0:T(8,128)(2,1)} async-done(((bf16[1,8192,128]{2,1,0:T(8,128)(2,1)}), bf16[1,1024,128]{2,1,0:T(8,128)(2,1)}) %reduce-scatter.7.cloned.1.call-update) | async-done | bytes 262160 | tf_op jit(solution)/shard_map/reduce_scatter | solution.py:133
  679.5 34.6 %reduce-scatter.9.cloned.1.call-done = bf16[1,1024,128]{2,1,0:T(8,128)(2,1)} async-done(((bf16[1,8192,128]{2,1,0:T(8,128)(2,1)}), bf16[1,1024,128]{2,1,0:T(8,128)(2,1)}) %reduce-scatter.9.cloned.1.call-update) | async-done | bytes 262160 | tf_op jit(solution)/shard_map/reduce_scatter | solution.py:136
  715.9 35.0 %reduce-scatter.11.cloned.1.call-done = bf16[1,1024,128]{2,1,0:T(8,128)(2,1)} async-done(((bf16[1,8192,128]{2,1,0:T(8,128)(2,1)}), bf16[1,1024,128]{2,1,0:T(8,128)(2,1)}) %reduce-scatter.11.cloned.1.call-update) | async-done | bytes 262160 | tf_op jit(solution)/shard_map/reduce_scatter | solution.py:139
  (354 shorter events, 396.9 us)
Async XLA Ops:
  7.2 8.5 %copy-start.9 = (bf16[1,1024,128]{2,1,0:T(8,128)(2,1)S(1)}, bf16[1,1024,128]{2,1,0:T(8,128)(2,1)}, u32[]{:S(2)}) copy-start(bf16[1,1024,128]{2,1,0:T(8,128)(2,1)} %param.21) | copy-start | bytes 786436
  7.2 47.7 %all-gather.4.cloned.1.call-start = ((), (), s32[]{:S(2)}) async-start(), calls=%async_computation.4 | async-start | bytes 2359296 | tf_op jit(solution)/shard_map/all_gather | solution.py:58
  7.9 73.1 %all-gather.6.cloned.1.call-start = ((), (), s32[]{:S(2)}) async-start(), calls=%async_computation.5 | async-start | bytes 2359296 | tf_op jit(solution)/shard_map/all_gather | solution.py:59
  8.7 102.6 %all-gather.8.cloned.1.call-start = ((), (), s32[]{:S(2)}) async-start(), calls=%async_computation.6 | async-start | bytes 2359296 | tf_op jit(solution)/shard_map/all_gather | solution.py:60
  9.4 631.8 %reduce-scatter.5.cloned.1.call-start = ((), (), s32[]{:S(2)}) async-start(), calls=%async_computation.7 | async-start | bytes 2359296 | tf_op jit(solution)/shard_map/reduce_scatter | solution.py:130
  9.4 9.0 %collective-permute-start.2 = (bf16[1,1024,128]{2,1,0:T(8,128)(2,1)}, bf16[1,1024,128]{2,1,0:T(8,128)(2,1)S(1)}, u32[]{:S(2)}, u32[]{:S(2)}) collective-permute-start(bf16[1,1024,128]{2,1,0:T(8,128)(2,1)} %param.21), channel_id=1, source_target_pairs={{0,1},{1,2},{2,3},{3,4},{4,5},{5,6},{6,7},{7,0},{8,9},{9,10},{10,1... | collective-permute-start | bytes 786440 | tf_op jit(solution)/shard_map/ppermute | solution.py:16
  9.9 9.1 %collective-permute-start.3 = (bf16[1,1024,128]{2,1,0:T(8,128)(2,1)}, bf16[1,1024,128]{2,1,0:T(8,128)(2,1)S(1)}, u32[]{:S(2)}, u32[]{:S(2)}) collective-permute-start(bf16[1,1024,128]{2,1,0:T(8,128)(2,1)} %param.21), channel_id=1, source_target_pairs={{0,7},{1,0},{2,1},{3,2},{4,3},{5,4},{6,5},{7,6},{8,15},{9,8},{10,9... | collective-permute-start | bytes 786440 | tf_op jit(solution)/shard_map/ppermute | solution.py:21
  18.4 11.8 %collective-permute-start.4 = (bf16[1,1024,128]{2,1,0:T(8,128)(2,1)S(1)}, bf16[1,1024,128]{2,1,0:T(8,128)(2,1)S(1)}, u32[]{:S(2)}, u32[]{:S(2)}) collective-permute-start(bf16[1,1024,128]{2,1,0:T(8,128)(2,1)S(1)} %collective-permute-done.2), channel_id=1, source_target_pairs={{0,1},{1,2},{2,3},{3,4},{4,5},{5,6},{6,7},{7,0},{8,9},{9,10},{10,1... | collective-permute-start | bytes 786440 | tf_op jit(solution)/shard_map/ppermute | solution.py:16
  19.0 15.0 %collective-permute-start.5 = (bf16[1,1024,128]{2,1,0:T(8,128)(2,1)S(1)}, bf16[1,1024,128]{2,1,0:T(8,128)(2,1)S(1)}, u32[]{:S(2)}, u32[]{:S(2)}) collective-permute-start(bf16[1,1024,128]{2,1,0:T(8,128)(2,1)S(1)} %collective-permute-done.3), channel_id=1, source_target_pairs={{0,7},{1,0},{2,1},{3,2},{4,3},{5,4},{6,5},{7,6},{8,15},{9,8},{10,9... | collective-permute-start | bytes 786440 | tf_op jit(solution)/shard_map/ppermute | solution.py:21
  30.2 13.5 %collective-permute-start.6 = (bf16[1,1024,128]{2,1,0:T(8,128)(2,1)S(1)}, bf16[1,1024,128]{2,1,0:T(8,128)(2,1)S(1)}, u32[]{:S(2)}, u32[]{:S(2)}) collective-permute-start(bf16[1,1024,128]{2,1,0:T(8,128)(2,1)S(1)} %collective-permute-done.4), channel_id=1, source_target_pairs={{0,1},{1,2},{2,3},{3,4},{4,5},{5,6},{6,7},{7,0},{8,9},{9,10},{10,1... | collective-permute-start | bytes 786440 | tf_op jit(solution)/shard_map/ppermute | solution.py:16
  34.0 14.2 %collective-permute-start.7 = (bf16[1,1024,128]{2,1,0:T(8,128)(2,1)S(1)}, bf16[1,1024,128]{2,1,0:T(8,128)(2,1)S(1)}, u32[]{:S(2)}, u32[]{:S(2)}) collective-permute-start(bf16[1,1024,128]{2,1,0:T(8,128)(2,1)S(1)} %collective-permute-done.5), channel_id=1, source_target_pairs={{0,7},{1,0},{2,1},{3,2},{4,3},{5,4},{6,5},{7,6},{8,15},{9,8},{10,9... | collective-permute-start | bytes 786440 | tf_op jit(solution)/shard_map/ppermute | solution.py:21
  39.2 73.7 %copy-start.10 = (s32[1,4,32]{2,1,0:T(4,128)S(1)}, s32[1,4,32]{2,1,0:T(4,128)}, u32[]{:S(2)}) copy-start(s32[1,4,32]{2,1,0:T(4,128)} %param.16) | copy-start | bytes 1540
  43.7 10.5 %collective-permute-start.8 = (bf16[1,1024,128]{2,1,0:T(8,128)(2,1)S(1)}, bf16[1,1024,128]{2,1,0:T(8,128)(2,1)S(1)}, u32[]{:S(2)}, u32[]{:S(2)}) collective-permute-start(bf16[1,1024,128]{2,1,0:T(8,128)(2,1)S(1)} %collective-permute-done.6), channel_id=1, source_target_pairs={{0,1},{1,2},{2,3},{3,4},{4,5},{5,6},{6,7},{7,0},{8,9},{9,10},{10,1... | collective-permute-start | bytes 786440 | tf_op jit(solution)/shard_map/ppermute | solution.py:16
  54.9 58.0 %copy-start = (bf16[1,8192,128]{2,1,0:T(8,128)(2,1)S(1)}, bf16[1,8192,128]{2,1,0:T(8,128)(2,1)}, u32[]{:S(2)}) copy-start(bf16[1,8192,128]{2,1,0:T(8,128)(2,1)} %all-gather.4.cloned.1.call-done) | copy-start | bytes 6291460
  124.6 13.4 %collective-permute-start = (bf16[32,8192]{1,0:T(8,128)(2,1)}, bf16[32,8192]{1,0:T(8,128)(2,1)S(1)}, u32[]{:S(2)}, u32[]{:S(2)}) collective-permute-start(bf16[32,8192]{1,0:T(8,128)(2,1)} %copy-done.8), channel_id=1, source_target_pairs={{0,8},{8,16},{16,24},{1,9},{9,17},{17,25},{2,10},{10,18},{18,26},{... | collective-permute-start | bytes 1572872 | tf_op jit(solution)/shard_map/while/body/eval_jaxpr/ppermute | solution.py:31
  149.7 15.6 %collective-permute-start = (bf16[32,8192]{1,0:T(8,128)(2,1)}, bf16[32,8192]{1,0:T(8,128)(2,1)S(1)}, u32[]{:S(2)}, u32[]{:S(2)}) collective-permute-start(bf16[32,8192]{1,0:T(8,128)(2,1)} %copy-done.8), channel_id=1, source_target_pairs={{0,8},{8,16},{16,24},{1,9},{9,17},{17,25},{2,10},{10,18},{18,26},{... | collective-permute-start | bytes 1572872 | tf_op jit(solution)/shard_map/while/body/eval_jaxpr/ppermute | solution.py:31
  177.0 14.8 %collective-permute-start = (bf16[32,8192]{1,0:T(8,128)(2,1)}, bf16[32,8192]{1,0:T(8,128)(2,1)S(1)}, u32[]{:S(2)}, u32[]{:S(2)}) collective-permute-start(bf16[32,8192]{1,0:T(8,128)(2,1)} %copy-done.8), channel_id=1, source_target_pairs={{0,8},{8,16},{16,24},{1,9},{9,17},{17,25},{2,10},{10,18},{18,26},{... | collective-permute-start | bytes 1572872 | tf_op jit(solution)/shard_map/while/body/eval_jaxpr/ppermute | solution.py:31
  203.5 13.8 %collective-permute-start = (bf16[32,8192]{1,0:T(8,128)(2,1)}, bf16[32,8192]{1,0:T(8,128)(2,1)S(1)}, u32[]{:S(2)}, u32[]{:S(2)}) collective-permute-start(bf16[32,8192]{1,0:T(8,128)(2,1)} %copy-done.8), channel_id=1, source_target_pairs={{0,8},{8,16},{16,24},{1,9},{9,17},{17,25},{2,10},{10,18},{18,26},{... | collective-permute-start | bytes 1572872 | tf_op jit(solution)/shard_map/while/body/eval_jaxpr/ppermute | solution.py:31
  221.3 21.3 %collective-permute-start = (bf16[32,8192]{1,0:T(8,128)(2,1)}, bf16[32,8192]{1,0:T(8,128)(2,1)S(1)}, u32[]{:S(2)}, u32[]{:S(2)}) collective-permute-start(bf16[32,8192]{1,0:T(8,128)(2,1)} %copy-done.8), channel_id=1, source_target_pairs={{0,8},{8,16},{16,24},{1,9},{9,17},{17,25},{2,10},{10,18},{18,26},{... | collective-permute-start | bytes 1572872 | tf_op jit(solution)/shard_map/while/body/eval_jaxpr/ppermute | solution.py:31
  246.6 13.2 %collective-permute-start = (bf16[32,8192]{1,0:T(8,128)(2,1)}, bf16[32,8192]{1,0:T(8,128)(2,1)S(1)}, u32[]{:S(2)}, u32[]{:S(2)}) collective-permute-start(bf16[32,8192]{1,0:T(8,128)(2,1)} %copy-done.8), channel_id=1, source_target_pairs={{0,8},{8,16},{16,24},{1,9},{9,17},{17,25},{2,10},{10,18},{18,26},{... | collective-permute-start | bytes 1572872 | tf_op jit(solution)/shard_map/while/body/eval_jaxpr/ppermute | solution.py:31
  263.7 20.0 %collective-permute-start = (bf16[32,8192]{1,0:T(8,128)(2,1)}, bf16[32,8192]{1,0:T(8,128)(2,1)S(1)}, u32[]{:S(2)}, u32[]{:S(2)}) collective-permute-start(bf16[32,8192]{1,0:T(8,128)(2,1)} %copy-done.8), channel_id=1, source_target_pairs={{0,8},{8,16},{16,24},{1,9},{9,17},{17,25},{2,10},{10,18},{18,26},{... | collective-permute-start | bytes 1572872 | tf_op jit(solution)/shard_map/while/body/eval_jaxpr/ppermute | solution.py:31
  295.0 18.3 %collective-permute-start.1 = (bf16[32,8192]{1,0:T(8,128)(2,1)S(1)}, bf16[32,8192]{1,0:T(8,128)(2,1)S(1)}, u32[]{:S(2)}, u32[]{:S(2)}) collective-permute-start(bf16[32,8192]{1,0:T(8,128)(2,1)S(1)} %get-tuple-element.1017), channel_id=1, source_target_pairs={{8,0},{16,8},{24,16},{9,1},{17,9},{25,17},{10,2},{18,10},{26,18},{... | collective-permute-start | bytes 1572872 | tf_op jit(solution)/shard_map/while/body/eval_jaxpr/ppermute | solution.py:31
  323.1 23.1 %collective-permute-start.1 = (bf16[32,8192]{1,0:T(8,128)(2,1)S(1)}, bf16[32,8192]{1,0:T(8,128)(2,1)S(1)}, u32[]{:S(2)}, u32[]{:S(2)}) collective-permute-start(bf16[32,8192]{1,0:T(8,128)(2,1)S(1)} %get-tuple-element.1017), channel_id=1, source_target_pairs={{8,0},{16,8},{24,16},{9,1},{17,9},{25,17},{10,2},{18,10},{26,18},{... | collective-permute-start | bytes 1572872 | tf_op jit(solution)/shard_map/while/body/eval_jaxpr/ppermute | solution.py:31
  355.9 46.7 %collective-permute-start.1 = (bf16[32,8192]{1,0:T(8,128)(2,1)S(1)}, bf16[32,8192]{1,0:T(8,128)(2,1)S(1)}, u32[]{:S(2)}, u32[]{:S(2)}) collective-permute-start(bf16[32,8192]{1,0:T(8,128)(2,1)S(1)} %get-tuple-element.1017), channel_id=1, source_target_pairs={{8,0},{16,8},{24,16},{9,1},{17,9},{25,17},{10,2},{18,10},{26,18},{... | collective-permute-start | bytes 1572872 | tf_op jit(solution)/shard_map/while/body/eval_jaxpr/ppermute | solution.py:31
  421.0 4.0 copy-start.1
  428.6 23.7 %collective-permute-start.1 = (bf16[32,8192]{1,0:T(8,128)(2,1)S(1)}, bf16[32,8192]{1,0:T(8,128)(2,1)S(1)}, u32[]{:S(2)}, u32[]{:S(2)}) collective-permute-start(bf16[32,8192]{1,0:T(8,128)(2,1)S(1)} %get-tuple-element.1017), channel_id=1, source_target_pairs={{8,0},{16,8},{24,16},{9,1},{17,9},{25,17},{10,2},{18,10},{26,18},{... | collective-permute-start | bytes 1572872 | tf_op jit(solution)/shard_map/while/body/eval_jaxpr/ppermute | solution.py:31
  478.2 23.7 %collective-permute-start.1 = (bf16[32,8192]{1,0:T(8,128)(2,1)S(1)}, bf16[32,8192]{1,0:T(8,128)(2,1)S(1)}, u32[]{:S(2)}, u32[]{:S(2)}) collective-permute-start(bf16[32,8192]{1,0:T(8,128)(2,1)S(1)} %get-tuple-element.1017), channel_id=1, source_target_pairs={{8,0},{16,8},{24,16},{9,1},{17,9},{25,17},{10,2},{18,10},{26,18},{... | collective-permute-start | bytes 1572872 | tf_op jit(solution)/shard_map/while/body/eval_jaxpr/ppermute | solution.py:31
  527.9 23.7 %collective-permute-start.1 = (bf16[32,8192]{1,0:T(8,128)(2,1)S(1)}, bf16[32,8192]{1,0:T(8,128)(2,1)S(1)}, u32[]{:S(2)}, u32[]{:S(2)}) collective-permute-start(bf16[32,8192]{1,0:T(8,128)(2,1)S(1)} %get-tuple-element.1017), channel_id=1, source_target_pairs={{8,0},{16,8},{24,16},{9,1},{17,9},{25,17},{10,2},{18,10},{26,18},{... | collective-permute-start | bytes 1572872 | tf_op jit(solution)/shard_map/while/body/eval_jaxpr/ppermute | solution.py:31
  577.6 23.1 %collective-permute-start.1 = (bf16[32,8192]{1,0:T(8,128)(2,1)S(1)}, bf16[32,8192]{1,0:T(8,128)(2,1)S(1)}, u32[]{:S(2)}, u32[]{:S(2)}) collective-permute-start(bf16[32,8192]{1,0:T(8,128)(2,1)S(1)} %get-tuple-element.1017), channel_id=1, source_target_pairs={{8,0},{16,8},{24,16},{9,1},{17,9},{25,17},{10,2},{18,10},{26,18},{... | collective-permute-start | bytes 1572872 | tf_op jit(solution)/shard_map/while/body/eval_jaxpr/ppermute | solution.py:31
  605.2 72.5 %reduce-scatter.7.cloned.1.call-start = ((), (), s32[]{:S(2)}) async-start(), calls=%async_computation.8 | async-start | bytes 2359296 | tf_op jit(solution)/shard_map/reduce_scatter | solution.py:133
  609.0 105.1 %reduce-scatter.9.cloned.1.call-start = ((), (), s32[]{:S(2)}) async-start(), calls=%async_computation.9 | async-start | bytes 2359296 | tf_op jit(solution)/shard_map/reduce_scatter | solution.py:136
  612.8 138.0 %reduce-scatter.11.cloned.1.call-start = ((), (), s32[]{:S(2)}) async-start(), calls=%async_computation.10 | async-start | bytes 2359296 | tf_op jit(solution)/shard_map/reduce_scatter | solution.py:139
  (37 other events, 71.4 us)
Sparse Core Ops, SparseCore 0:
  9.6 40.9 all-gather.3
  52.2 28.7 all-gather.5
  82.7 28.5 all-gather.7
  605.3 35.8 reduce-scatter.4
  643.3 34.3 reduce-scatter.6
  679.8 34.2 reduce-scatter.8
  716.4 34.3 reduce-scatter.10
